TPU v7x, 32 devices: a whole 2x2x4 slice. The times are simulated.
32 devices in a mesh: req: 4 (over y, core), ad: 8 (over z, x).
Axes of the slice: x: 2, y: 2, z: 4, core: 2. Of those that a mesh axis runs over, the one named last changes fastest.
Arguments:
- residual: bfloat16 [256, 32, 1152], P(('req', 'ad')), may hold values from -16 to 16
- lengths: int32 [256], P(('req', 'ad')), may hold values from 1 to 32, 7168 in all
- adapter_ids: int32 [256], P(('req', 'ad')), may hold values from 0 to 31, as said below
- ffn_gain: float32 [1152], replicated, may hold values from 0.5 to 1.5
- w_gate_up: bfloat16 [2, 1152, 3072], replicated, may hold values from -0.1875 to 0.1875
- w_down: bfloat16 [3072, 1152], replicated, may hold values from -0.109375 to 0.109375
- adapter_input_first: bfloat16 [32, 32, 1152], P('ad'), may hold values from -0.1875 to 0.1875
- ad_out_b: bfloat16 [32, 2, 16, 3072], P('ad'), may hold values from -1.5 to 1.5
- ad_down_a: bfloat16 [32, 16, 3072], P('ad'), may hold values from -0.109375 to 0.109375
- adapter_down_second: bfloat16 [32, 16, 1152], P('ad'), may hold values from -1.5 to 1.5
- final_gain: float32 [1152], replicated, may hold values from 0.5 to 1.5
- head_weight: bfloat16 [1152, 32000], P(None, ('req', 'ad')), may hold values from -3 to 3
Outputs:
- layer_out: bfloat16 [256, 32, 1152], P(('req', 'ad'))
- log_probs: float32 [256, 32000], P(None, ('req', 'ad'))
Inputs may be any that keep to these rules, and one draw needn't show every extreme that they name: `adapter_ids`: the 8 requests of one device (aligned blocks of 8 requests in order) use adapters whose indices divided by 4 are all different.
All inputs are finite; a program needn't handle non-finite values. No bound on the sum of `lengths` on one device may be relied on, other than what follows from the above.
Results may differ from a plain program's by a relative error of at most 0.0076.
Values may be sent and summed in bfloat16 or wider, within the bound.
A program may use at most 128 MiB of HBM per device.

v0:
```python
import jax
import jax.numpy as jnp
from jax import lax
from jax.sharding import PartitionSpec as P

epsilon = 1e-05


def rms_scale(values, gain):
    mean_sq = jnp.mean(values * values, axis=-1, keepdims=True)
    return values * lax.rsqrt(mean_sq + epsilon) * gain


def picks_of(slot_ids, per_dev):
    return (slot_ids[..., None] == jnp.arange(per_dev, dtype=jnp.int32)).astype(jnp.float32)


def adapter_gate_up(row_block, picks, in_a, out_b):
    lowered = jnp.einsum("isd,akd->isak", row_block, in_a, preferred_element_type=jnp.float32)
    input_lowrank_state = jnp.sum(lowered * picks[..., None], axis=2).astype(jnp.bfloat16)
    spread = input_lowrank_state[:, :, None, :] * picks[..., None].astype(jnp.bfloat16)
    rank = out_b.shape[2]
    spread = spread.reshape(spread.shape[0], spread.shape[1], spread.shape[2], 2, rank)
    return jnp.einsum("isajr,ajrf->isjf", spread, out_b, preferred_element_type=jnp.float32).astype(
        jnp.bfloat16
    )


def adapter_down(hidden_block, picks, down_a, down_b):
    lowered = jnp.einsum("isf,akf->isak", hidden_block, down_a, preferred_element_type=jnp.float32)
    down_lowrank_state = jnp.sum(lowered * picks[..., None], axis=2).astype(jnp.bfloat16)
    spread = down_lowrank_state[:, :, None, :] * picks[..., None].astype(jnp.bfloat16)
    return jnp.einsum("isak,akd->isd", spread, down_b, preferred_element_type=jnp.float32).astype(
        jnp.bfloat16
    )


def base_gate_up(normalized_rows, w_gate_up):
    lead = normalized_rows.shape[:-1]
    flat = normalized_rows.reshape(-1, normalized_rows.shape[-1])
    gate = jnp.dot(flat, w_gate_up[0], preferred_element_type=jnp.float32)
    up_part = jnp.dot(flat, w_gate_up[1], preferred_element_type=jnp.float32)
    return (gate.reshape(lead + (gate.shape[-1],)), up_part.reshape(lead + (up_part.shape[-1],)))


def base_down(hidden, w_down):
    lead = hidden.shape[:-1]
    result = jnp.dot(
        hidden.reshape(-1, hidden.shape[-1]), w_down, preferred_element_type=jnp.float32
    )
    return result.reshape(lead + (result.shape[-1],))


def local(
    residual,
    lengths,
    adapter_ids,
    ffn_gain,
    w_gate_up,
    w_down,
    adapter_input_first,
    ad_out_b,
    ad_down_a,
    adapter_down_second,
    final_gain,
    head_weight,
):
    req_dev, seq_len, width = residual.shape
    groups = lax.axis_size("ad")
    per_dev = adapter_input_first.shape[0]
    positions = jnp.arange(seq_len, dtype=jnp.int32)
    valid = positions[None, :] < lengths[:, None]
    stream = residual.astype(jnp.float32)
    normalized_rows = rms_scale(stream, ffn_gain).astype(jnp.bfloat16)
    kept = jnp.where(valid[..., None], normalized_rows, jnp.zeros_like(normalized_rows))
    holder = adapter_ids // per_dev
    local_id = adapter_ids % per_dev
    placing = jnp.arange(groups, dtype=jnp.int32)[:, None] == holder[None, :]
    place_bf = placing.astype(jnp.bfloat16)
    slot_ids = jnp.sum(placing.astype(jnp.int32) * local_id[None, :], axis=1)
    slot_rows = jnp.broadcast_to(slot_ids[:, None], (groups, seq_len))

    def place(values):
        return jnp.einsum(
            "hr,rsf->hsf", place_bf, values, preferred_element_type=jnp.float32
        ).astype(jnp.bfloat16)

    def unplace(returned):
        return jnp.einsum("hr,hsf->rsf", place_bf, returned, preferred_element_type=jnp.float32)

    row_block = lax.all_to_all(place(kept), "ad", split_axis=0, concat_axis=0, tiled=True)
    row_ids = lax.all_to_all(slot_rows, "ad", split_axis=0, concat_axis=0, tiled=True)
    delta = adapter_gate_up(row_block, picks_of(row_ids, per_dev), adapter_input_first, ad_out_b)
    delta = delta.reshape(delta.shape[0], delta.shape[1], -1)
    returned_gu = lax.all_to_all(delta, "ad", split_axis=0, concat_axis=0, tiled=True)
    gate, up_part = base_gate_up(normalized_rows, w_gate_up)
    hidden_units = gate.shape[-1]
    delta_gu = unplace(returned_gu)
    hidden = (
        jax.nn.silu(gate + delta_gu[..., :hidden_units]) * (up_part + delta_gu[..., hidden_units:])
    ).astype(jnp.bfloat16)
    hidden_kept = jnp.where(valid[..., None], hidden, jnp.zeros_like(hidden))
    hidden_block = lax.all_to_all(place(hidden_kept), "ad", split_axis=0, concat_axis=0, tiled=True)
    row_ids = lax.all_to_all(slot_rows, "ad", split_axis=0, concat_axis=0, tiled=True)
    delta = adapter_down(hidden_block, picks_of(row_ids, per_dev), ad_down_a, adapter_down_second)
    returned_down = lax.all_to_all(delta, "ad", split_axis=0, concat_axis=0, tiled=True)
    mixed = stream + base_down(hidden, w_down) + unplace(returned_down)
    layer_out = jnp.where(valid[..., None], mixed, jnp.zeros_like(mixed)).astype(jnp.bfloat16)
    last_index = (lengths - 1)[:, None, None]
    last_row = jnp.take_along_axis(layer_out, last_index, axis=1)[:, 0, :].astype(jnp.float32)
    final = rms_scale(last_row, final_gain).astype(jnp.bfloat16)
    logits = jnp.dot(
        lax.all_gather(final, ("req", "ad"), axis=0, tiled=True),
        head_weight,
        preferred_element_type=jnp.float32,
    )
    local_max = jnp.max(logits, axis=1)
    highest = lax.pmax(local_max, ("req", "ad"))
    total = lax.psum(jnp.sum(jnp.exp(logits - highest[:, None]), axis=1), ("req", "ad"))
    log_probs = logits - highest[:, None] - jnp.log(total)[:, None]
    return (layer_out, log_probs)


def solution(mesh):
    in_specs = (
        P(("req", "ad"), None, None),
        P(("req", "ad")),
        P(("req", "ad")),
        P(),
        P(),
        P(),
        P("ad", None, None),
        P("ad", None, None, None),
        P("ad", None, None),
        P("ad", None, None),
        P(),
        P(None, ("req", "ad")),
    )
    out_specs = (P(("req", "ad"), None, None), P(None, ("req", "ad")))
    return jax.shard_map(local, mesh=mesh, in_specs=in_specs, out_specs=out_specs, check_vma=False)
```

profile of v0, /device:TPU:0, one launch (start us, length us, event | category | flops | bytes accessed | tf_op | source)
XLA Modules:
  0.0 355.6 jit_solution(7166750114568926179)
XLA Ops:
  0.6 0.8 and_select_fusion.1
  1.5 0.1 select_reduce_fusion
  1.5 0.7 broadcast_in_dim.35
  2.2 7.3 %all-to-all-start.1 = ((s32[8,1,32]{2,1,0:T(1,128)}), s32[8,1,32]{2,1,0:T(1,128)S(1)}, u32[]{:S(2)}, u32[]{:S(2)}) async-start(s32[8,1,32]{2,1,0:T(1,128)} %broadcast_in_dim.35), calls=%async_computation.1 | async-start | bytes 8192 | tf_op jit(solution)/shard_map/all_to_all | solution.py:92
  9.5 1.2 fusion.40
  10.7 0.7 iota_compare_fusion.2
  11.5 1.4 broadcast_select_fusion.1
  12.9 0.4 convolution_convert_fusion.1
  13.3 0.9 copy.48
  14.2 1.7 all-to-all-done.1
  15.9 4.3 %all-to-all-start = ((bf16[8,32,1152]{2,1,0:T(8,128)(2,1)}), bf16[8,32,1152]{2,1,0:T(8,128)(2,1)}, u32[]{:S(2)}, u32[]{:S(2)}) async-start(bf16[8,32,1152]{2,1,0:T(8,128)(2,1)} %copy.48), calls=%async_computation | async-start | bytes 1179648 | tf_op jit(solution)/shard_map/all_to_all | solution.py:91
  20.2 15.5 %all-to-all-done = bf16[8,32,1152]{2,1,0:T(8,128)(2,1)} async-done(((bf16[8,32,1152]{2,1,0:T(8,128)(2,1)}), bf16[8,32,1152]{2,1,0:T(8,128)(2,1)}, u32[]{:S(2)}, u32[]{:S(2)}) %all-to-all-start) | async-done | bytes 589856 | tf_op jit(solution)/shard_map/all_to_all | solution.py:91
  35.7 1.6 fusion.39
  37.3 0.1 copy.49
  37.4 1.0 fusion.8
  38.4 0.3 copy.84
  38.7 74.3 %all_to_all.27 = bf16[8,32,6144]{2,1,0:T(8,128)(2,1)S(1)} all-to-all(bf16[8,32,6144]{2,1,0:T(8,128)(2,1)S(1)} %bitcast.85), channel_id=1, replica_groups=mesh['req'=4,'ad'=8] {'ad'}, dimensions={0} | all-to-all | bytes 6291456 | tf_op jit(solution)/shard_map/all_to_all | solution.py:95
  113.0 3.5 fusion.21
  116.6 0.7 fusion.74
  117.3 0.3 copy-done.1
  117.6 0.5 slice-done.3
  118.1 3.9 %fusion.9 = f32[8,32,3072]{2,1,0:T(8,128)S(1)} fusion(bf16[2,1152,3072]{2,1,0:T(8,128)(2,1)S(1)} %bitcast.89, f32[8,32,3072]{2,0,1:T(8,128)S(1)} %get-tuple-element.2, bf16[8,32,1152]{2,1,0:T(8,128)(2,1)S(1)} %copy-done.1, f32[1152]{0:T(1024)S(1)} %copy-done.4, f32[8,32]{1,0:T(8,128)S(1)} %add_rsqrt_fusion), kind=kOutput, calls=%fused_computation.11 | convolution fusion | flops 1813905408 | bytes 13971456 | tf_op jit(solution)/shard_map/dot_general | solution.py:41
  122.1 5.1 %broadcast_select_fusion = (bf16[8,32,3072]{2,1,0:T(8,128)(2,1)S(1)}, bf16[8,32,3072]{2,1,0:T(8,128)(2,1)}) fusion(pred[8,32]{1,0:T(8,128)(4,1)S(1)} %iota_compare_fusion.2, f32[8,32,3072]{2,0,1:T(8,128)S(1)} %get-tuple-element.3, bf16[2,1152,3072]{2,1,0:T(8,128)(2,1)S(1)} %bitcast.89, bf16[8,32,1152]{2,1,0:T(8,128)(2,1)S(1)} %copy-done.1, ...), kind=kOutput, calls=%fused_computation.30 | convolution fusion | flops 1819410432 | bytes 17118208 | tf_op jit(solution)/shard_map/dot_general | solution.py:42
  127.2 1.2 convolution_convert_fusion
  128.4 2.0 copy.58
  130.4 4.5 %all-to-all-start.3 = ((bf16[8,32,3072]{2,1,0:T(8,128)(2,1)}), bf16[8,32,3072]{2,1,0:T(8,128)(2,1)}, u32[]{:S(2)}, u32[]{:S(2)}) async-start(bf16[8,32,3072]{2,1,0:T(8,128)(2,1)} %copy.58), calls=%async_computation.3 | async-start | bytes 3145728 | tf_op jit(solution)/shard_map/all_to_all | solution.py:103
  134.9 0.1 copy.60
  135.0 0.7 copy.63
  135.8 35.1 %all-to-all-done.3 = bf16[8,32,3072]{2,1,0:T(8,128)(2,1)} async-done(((bf16[8,32,3072]{2,1,0:T(8,128)(2,1)}), bf16[8,32,3072]{2,1,0:T(8,128)(2,1)}, u32[]{:S(2)}, u32[]{:S(2)}) %all-to-all-start.3) | async-done | bytes 1572896 | tf_op jit(solution)/shard_map/all_to_all | solution.py:103
  170.8 3.6 %fusion.36 = f32[8,32,4,16]{1,3,2,0:T(8,128)} fusion(bf16[8,32,3072]{2,1,0:T(8,128)(2,1)} %all-to-all-done.3, bf16[4,16,3072]{2,1,0:T(8,128)(2,1)} %param.20), kind=kOutput, calls=%fused_computation.27 | convolution fusion | flops 100663296 | bytes 2031616 | tf_op jit(solution)/shard_map/isf,akf->isak/dot_general | solution.py:30
  174.4 1.4 copy.73
  175.8 0.2 multiply_reduce_fusion
  176.1 0.1 copy.81
  176.2 0.1 copy.62
  176.3 1.5 fusion.32
  177.8 0.9 copy.64
  178.7 3.6 %all-to-all-start.4 = ((bf16[8,32,1152]{2,1,0:T(8,128)(2,1)}), bf16[8,32,1152]{2,1,0:T(8,128)(2,1)S(1)}, u32[]{:S(2)}, u32[]{:S(2)}) async-start(bf16[8,32,1152]{2,1,0:T(8,128)(2,1)} %copy.64), calls=%async_computation.4 | async-start | bytes 1179648 | tf_op jit(solution)/shard_map/all_to_all | solution.py:106
  182.3 16.0 %all-to-all-done.4 = bf16[8,32,1152]{2,1,0:T(8,128)(2,1)S(1)} async-done(((bf16[8,32,1152]{2,1,0:T(8,128)(2,1)}), bf16[8,32,1152]{2,1,0:T(8,128)(2,1)S(1)}, u32[]{:S(2)}, u32[]{:S(2)}) %all-to-all-start.4) | async-done | bytes 589856 | tf_op jit(solution)/shard_map/all_to_all | solution.py:106
  198.3 0.4 fusion.45
  198.7 5.9 %fusion.33 = bf16[8,32,1152]{2,1,0:T(8,128)(2,1)S(1)} fusion(bf16[8,32,3072]{2,1,0:T(8,128)(2,1)} %get-tuple-element.9, bf16[3072,1152]{1,0:T(8,128)(2,1)} %param.17, bf16[8,32,1152]{2,1,0:T(8,128)(2,1)S(1)} %copy-done.1, f32[8,32,1152]{2,0,1:T(8,128)S(1)} %fusion.45, pred[8,32]{1,0:T(8,128)(4,1)S(1)} %copy-done.7), kind=kOutput, calls=%fused_computation.23 | convolution fusion | flops 1813413888 | bytes 11010304 | tf_op jit(solution)/shard_map/dot_general | solution.py:48
  204.6 0.6 gather_fusion
  205.3 0.2 fusion.59
  205.6 69.7 %all_gather.3 = bf16[256,1152]{1,0:T(8,128)(2,1)S(1)} all-gather(bf16[8,1152]{1,0:T(8,128)(2,1)S(1)} %fusion.61), channel_id=1, replica_groups=mesh['req'=4,'ad'=8] {'req','ad'}, dimensions={0}, use_global_device_ids=true | all-gather | bytes 608256 | tf_op jit(solution)/shard_map/all_gather | solution.py:113
  275.2 0.9 fusion.75
  276.2 36.9 %pmax.7 = f32[256]{0:T(256)S(1)} all-reduce(f32[256]{0:T(256)S(1)} %get-tuple-element.10), channel_id=1, replica_groups=mesh['req'=4,'ad'=8] {'req','ad'}, use_global_device_ids=true, to_apply=%region_6.7 | all-reduce | flops 256 | bytes 2048 | tf_op jit(solution)/shard_map/pmax | solution.py:118
  313.0 0.2 exponential_reduce_fusion
  313.3 41.3 %psum.7 = f32[256]{0:T(256)S(1)} all-reduce(f32[256]{0:T(256)S(1)} %exponential_reduce_fusion), channel_id=1, replica_groups=mesh['req'=4,'ad'=8] {'req','ad'}, use_global_device_ids=true, to_apply=%region_8.9 | all-reduce | flops 256 | bytes 2048 | tf_op jit(solution)/shard_map/psum | solution.py:119
  354.6 1.0 subtract_subtract_fusion
  (37 shorter events, 0.2 us)
Async XLA Ops:
  0.6 274.6 %copy-start = (bf16[1152,1000]{0,1:T(8,128)(2,1)S(1)}, bf16[1152,1000]{0,1:T(8,128)(2,1)}, u32[]{:S(2)}) copy-start(bf16[1152,1000]{0,1:T(8,128)(2,1)} %param.23) | copy-start | bytes 6912004
  2.2 13.6 %all-to-all-start.1 = ((s32[8,1,32]{2,1,0:T(1,128)}), s32[8,1,32]{2,1,0:T(1,128)S(1)}, u32[]{:S(2)}, u32[]{:S(2)}) async-start(s32[8,1,32]{2,1,0:T(1,128)} %broadcast_in_dim.35), calls=%async_computation.1 | async-start | bytes 8192 | tf_op jit(solution)/shard_map/all_to_all | solution.py:92
  11.5 110.6 %copy-start.6 = (pred[8,32]{1,0:T(8,128)(4,1)}, pred[8,32]{1,0:T(8,128)(4,1)S(1)}, u32[]{:S(2)}) copy-start(pred[8,32]{1,0:T(8,128)(4,1)S(1)} %iota_compare_fusion.2) | copy-start | bytes 772
  11.5 24.2 %copy-start.8 = (bf16[4,32,1152]{2,1,0:T(8,128)(2,1)S(1)}, bf16[4,32,1152]{2,1,0:T(8,128)(2,1)}, u32[]{:S(2)}) copy-start(bf16[4,32,1152]{2,1,0:T(8,128)(2,1)} %param.18) | copy-start | bytes 884740
  13.3 24.1 %copy-start.2 = (bf16[4,2,16,3072]{3,2,1,0:T(8,128)(2,1)S(1)}, bf16[4,2,16,3072]{3,2,1,0:T(8,128)(2,1)}, u32[]{:S(2)}) copy-start(bf16[4,2,16,3072]{3,2,1,0:T(8,128)(2,1)} %param.19) | copy-start | bytes 2359300
  15.9 19.8 %all-to-all-start = ((bf16[8,32,1152]{2,1,0:T(8,128)(2,1)}), bf16[8,32,1152]{2,1,0:T(8,128)(2,1)}, u32[]{:S(2)}, u32[]{:S(2)}) async-start(bf16[8,32,1152]{2,1,0:T(8,128)(2,1)} %copy.48), calls=%async_computation | async-start | bytes 1179648 | tf_op jit(solution)/shard_map/all_to_all | solution.py:91
  38.4 78.9 %slice-start = ((s8[14155776]{0:T(1024)(128)(4,1)}), s8[4194304]{0:T(1024)(128)(4,1)S(1)}, s32[]{:S(2)}) async-start(s8[14155776]{0:T(1024)(128)(4,1)} %bitcast.88), calls=%async_computation.5 | async-start | bytes 8388608
  38.7 78.6 %slice-start.1 = ((s8[14155776]{0:T(1024)(128)(4,1)}), s8[4194304]{0:T(1024)(128)(4,1)S(1)}, s32[]{:S(2)}) async-start(s8[14155776]{0:T(1024)(128)(4,1)} %bitcast.88), calls=%async_computation.6 | async-start | bytes 8388608
  113.0 4.3 %slice-start.2 = ((s8[14155776]{0:T(1024)(128)(4,1)}), s8[4194304]{0:T(1024)(128)(4,1)S(1)}, s32[]{:S(2)}) async-start(s8[14155776]{0:T(1024)(128)(4,1)} %bitcast.88), calls=%async_computation.7 | async-start | bytes 8388608
  116.5 1.1 copy-start.1
  116.5 1.1 copy-start.4
  116.6 1.6 slice-start.3
  130.4 40.4 %all-to-all-start.3 = ((bf16[8,32,3072]{2,1,0:T(8,128)(2,1)}), bf16[8,32,3072]{2,1,0:T(8,128)(2,1)}, u32[]{:S(2)}, u32[]{:S(2)}) async-start(bf16[8,32,3072]{2,1,0:T(8,128)(2,1)} %copy.58), calls=%async_computation.3 | async-start | bytes 3145728 | tf_op jit(solution)/shard_map/all_to_all | solution.py:103
  176.3 6.0 %copy-start.9 = (s32[8]{0:T(128)S(1)}, s32[8]{0:T(128)}, u32[]{:S(2)}) copy-start(s32[8]{0:T(128)} %param.13) | copy-start | bytes 100
  177.8 20.9 %copy-start.7 = (pred[8,32]{1,0:T(8,128)(4,1)S(1)}, pred[8,32]{1,0:T(8,128)(4,1)}, u32[]{:S(2)}) copy-start(pred[8,32]{1,0:T(8,128)(4,1)} %copy-done.6) | copy-start | bytes 772
  178.7 19.6 %all-to-all-start.4 = ((bf16[8,32,1152]{2,1,0:T(8,128)(2,1)}), bf16[8,32,1152]{2,1,0:T(8,128)(2,1)S(1)}, u32[]{:S(2)}, u32[]{:S(2)}) async-start(bf16[8,32,1152]{2,1,0:T(8,128)(2,1)} %copy.64), calls=%async_computation.4 | async-start | bytes 1179648 | tf_op jit(solution)/shard_map/all_to_all | solution.py:106
  198.7 6.8 %copy-start.5 = (f32[1152]{0:T(1024)S(1)}, f32[1152]{0:T(1024)}, u32[]{:S(2)}) copy-start(f32[1152]{0:T(1024)} %param.22) | copy-start | bytes 13828
  204.6 0.9 copy-start.3
where the time goes:
time: 356 us
  blocking collectives  222 us (62%)
  waiting for transfers between devices  68.2 us (19%)
  matrix products  29 us (8%)
  starting transfers between devices  19.7 us (6%)
  local copies, waits for them, and re-layouts  9.53 us (3%)
  other arithmetic  6.06 us (2%)
    all_to_all x1, blocking collectives, local(): lax.all_to_all(delta, 'ad', split_axis=0, concat_axis=0, tiled=True)  74.3 us
    all_gather x1, blocking collectives, local(): lax.all_gather(final, ('req', 'ad'), axis=0, tiled=True)  69.7 us
    psum x1, blocking collectives, local(): lax.psum(jnp.sum(jnp.exp(logits - highest[:, None]), axis=1), ('req', 'ad'))  41.3 us
    pmax x1, blocking collectives, local(): highest = lax.pmax(local_max, ('req', 'ad'))  36.9 us
    all_to_all x1, waiting for transfers between devices, local(): lax.all_to_all(place(hidden_kept), 'ad', split_axis=0, concat_axis=0, til...  35.1 us
    all_to_all x1, waiting for transfers between devices, local(): lax.all_to_all(delta, 'ad', split_axis=0, concat_axis=0, tiled=True)  16 us
    all_to_all x1, waiting for transfers between devices, local(): lax.all_to_all(place(kept), 'ad', split_axis=0, concat_axis=0, tiled=True)  15.5 us
    all_to_all x1, starting transfers between devices, local(): lax.all_to_all(slot_rows, 'ad', split_axis=0, concat_axis=0, tiled=True)  7.25 us
  transfers between devices with their start and end apart: 4, of which 4 were waited for; matrix products, arithmetic and copies ran while one was open for 2% of the time, Pallas kernels for 0%

commit v1 on v0

--- a/solution.py
+++ b/solution.py
@@ -116,7 +116,7 @@
     )
     local_max = jnp.max(logits, axis=1)
     highest = lax.pmax(local_max, ("req", "ad"))
-    total = lax.psum(jnp.sum(jnp.exp(logits - highest[:, None]), axis=1), ("req", "ad"))
+    total = lax.psum(lax.psum(jnp.sum(jnp.exp(logits - highest[:, None]), axis=1), "ad"), "req")
     log_probs = logits - highest[:, None] - jnp.log(total)[:, None]
     return (layer_out, log_probs)
 

time: 356 us -> 342 us (0.961)
  blocking collectives: 222 us -> 208 us
    psum x1 -> x2, blocking collectives: 41.3 us -> 27 us  [the longest x1 21.1 us: local(): lax.psum(jnp.sum(jnp.exp(logits - highest[:, None]), axis=1), 'ad')]
where the time goes in v1:
time: 342 us; the launch traced here: 341 us
  blocking collectives  208 us (61%)
  waiting for transfers between devices  68.2 us (20%)
  matrix products  29 us (8%)
  starting transfers between devices  19.7 us (6%)
  local copies, waits for them, and re-layouts  9.53 us (3%)
  other arithmetic  6.06 us (2%)
    all_to_all x1, blocking collectives, local(): lax.all_to_all(delta, 'ad', split_axis=0, concat_axis=0, tiled=True)  74.3 us
    all_gather x1, blocking collectives, local(): lax.all_gather(final, ('req', 'ad'), axis=0, tiled=True)  69.7 us
    pmax x1, blocking collectives, local(): highest = lax.pmax(local_max, ('req', 'ad'))  36.9 us
    all_to_all x1, waiting for transfers between devices, local(): lax.all_to_all(place(hidden_kept), 'ad', split_axis=0, concat_axis=0, til...  35.1 us
    psum x1, blocking collectives, local(): lax.psum(jnp.sum(jnp.exp(logits - highest[:, None]), axis=1), 'ad')  21.1 us
    all_to_all x1, waiting for transfers between devices, local(): lax.all_to_all(delta, 'ad', split_axis=0, concat_axis=0, tiled=True)  16 us
    all_to_all x1, waiting for transfers between devices, local(): lax.all_to_all(place(kept), 'ad', split_axis=0, concat_axis=0, tiled=True)  15.5 us
    all_to_all x1, starting transfers between devices, local(): lax.all_to_all(slot_rows, 'ad', split_axis=0, concat_axis=0, tiled=True)  7.25 us
  transfers between devices with their start and end apart: 4, of which 4 were waited for; matrix products, arithmetic and copies ran while one was open for 2% of the time, Pallas kernels for 0%

profile of v1, /device:TPU:0, one launch (start us, length us, event | category | flops | bytes accessed | tf_op | source)
XLA Modules:
  0.0 341.3 jit_solution(4384944987308630732)
XLA Ops:
  0.6 0.8 and_select_fusion.1
  1.5 0.7 broadcast_in_dim.35
  2.2 7.3 %all-to-all-start.1 = ((s32[8,1,32]{2,1,0:T(1,128)}), s32[8,1,32]{2,1,0:T(1,128)S(1)}, u32[]{:S(2)}, u32[]{:S(2)}) async-start(s32[8,1,32]{2,1,0:T(1,128)} %broadcast_in_dim.35), calls=%async_computation.1 | async-start | bytes 8192 | tf_op jit(solution)/shard_map/all_to_all | solution.py:92
  9.5 1.2 fusion.40
  10.7 0.7 iota_compare_fusion.2
  11.5 1.4 broadcast_select_fusion.1
  12.9 0.4 convolution_convert_fusion.1
  13.3 0.9 copy.48
  14.2 1.7 all-to-all-done.1
  15.9 4.3 %all-to-all-start = ((bf16[8,32,1152]{2,1,0:T(8,128)(2,1)}), bf16[8,32,1152]{2,1,0:T(8,128)(2,1)}, u32[]{:S(2)}, u32[]{:S(2)}) async-start(bf16[8,32,1152]{2,1,0:T(8,128)(2,1)} %copy.48), calls=%async_computation | async-start | bytes 1179648 | tf_op jit(solution)/shard_map/all_to_all | solution.py:91
  20.2 15.5 %all-to-all-done = bf16[8,32,1152]{2,1,0:T(8,128)(2,1)} async-done(((bf16[8,32,1152]{2,1,0:T(8,128)(2,1)}), bf16[8,32,1152]{2,1,0:T(8,128)(2,1)}, u32[]{:S(2)}, u32[]{:S(2)}) %all-to-all-start) | async-done | bytes 589856 | tf_op jit(solution)/shard_map/all_to_all | solution.py:91
  35.7 1.6 fusion.39
  37.3 0.1 copy.49
  37.4 1.0 fusion.8
  38.4 0.3 copy.84
  38.7 74.3 %all_to_all.27 = bf16[8,32,6144]{2,1,0:T(8,128)(2,1)S(1)} all-to-all(bf16[8,32,6144]{2,1,0:T(8,128)(2,1)S(1)} %bitcast.85), channel_id=1, replica_groups=mesh['req'=4,'ad'=8] {'ad'}, dimensions={0} | all-to-all | bytes 6291456 | tf_op jit(solution)/shard_map/all_to_all | solution.py:95
  113.0 3.5 %fusion.21 = f32[8,32,6144]{2,0,1:T(8,128)S(1)} fusion(bf16[8,32,6144]{2,1,0:T(8,128)(2,1)S(1)} %all_to_all.27, s32[8]{0:T(128)S(1)} %get-tuple-element.6), kind=kOutput, calls=%fused_computation.16 | convolution fusion | flops 25165888 | bytes 9437216 | tf_op jit(solution)/shard_map/hr,hsf->rsf/dot_general | solution.py:89
  116.6 0.7 fusion.74
  117.3 0.3 copy-done.1
  117.6 0.5 slice-done.3
  118.1 3.9 %fusion.9 = f32[8,32,3072]{2,1,0:T(8,128)S(1)} fusion(bf16[2,1152,3072]{2,1,0:T(8,128)(2,1)S(1)} %bitcast.89, f32[8,32,3072]{2,0,1:T(8,128)S(1)} %get-tuple-element.2, bf16[8,32,1152]{2,1,0:T(8,128)(2,1)S(1)} %copy-done.1, f32[1152]{0:T(1024)S(1)} %copy-done.4, f32[8,32]{1,0:T(8,128)S(1)} %add_rsqrt_fusion), kind=kOutput, calls=%fused_computation.11 | convolution fusion | flops 1813905408 | bytes 13971456 | tf_op jit(solution)/shard_map/dot_general | solution.py:41
  122.1 5.1 %broadcast_select_fusion = (bf16[8,32,3072]{2,1,0:T(8,128)(2,1)S(1)}, bf16[8,32,3072]{2,1,0:T(8,128)(2,1)}) fusion(pred[8,32]{1,0:T(8,128)(4,1)S(1)} %iota_compare_fusion.2, f32[8,32,3072]{2,0,1:T(8,128)S(1)} %get-tuple-element.3, bf16[2,1152,3072]{2,1,0:T(8,128)(2,1)S(1)} %bitcast.89, bf16[8,32,1152]{2,1,0:T(8,128)(2,1)S(1)} %copy-done.1, ...), kind=kOutput, calls=%fused_computation.30 | convolution fusion | flops 1819410432 | bytes 17118208 | tf_op jit(solution)/shard_map/dot_general | solution.py:42
  127.2 1.2 convolution_convert_fusion
  128.4 2.0 copy.58
  130.4 4.5 %all-to-all-start.3 = ((bf16[8,32,3072]{2,1,0:T(8,128)(2,1)}), bf16[8,32,3072]{2,1,0:T(8,128)(2,1)}, u32[]{:S(2)}, u32[]{:S(2)}) async-start(bf16[8,32,3072]{2,1,0:T(8,128)(2,1)} %copy.58), calls=%async_computation.3 | async-start | bytes 3145728 | tf_op jit(solution)/shard_map/all_to_all | solution.py:103
  134.9 0.1 copy.60
  135.0 0.7 copy.63
  135.7 35.1 %all-to-all-done.3 = bf16[8,32,3072]{2,1,0:T(8,128)(2,1)} async-done(((bf16[8,32,3072]{2,1,0:T(8,128)(2,1)}), bf16[8,32,3072]{2,1,0:T(8,128)(2,1)}, u32[]{:S(2)}, u32[]{:S(2)}) %all-to-all-start.3) | async-done | bytes 1572896 | tf_op jit(solution)/shard_map/all_to_all | solution.py:103
  170.8 3.6 %fusion.36 = f32[8,32,4,16]{1,3,2,0:T(8,128)} fusion(bf16[8,32,3072]{2,1,0:T(8,128)(2,1)} %all-to-all-done.3, bf16[4,16,3072]{2,1,0:T(8,128)(2,1)} %param.20), kind=kOutput, calls=%fused_computation.27 | convolution fusion | flops 100663296 | bytes 2031616 | tf_op jit(solution)/shard_map/isf,akf->isak/dot_general | solution.py:30
  174.4 1.4 copy.73
  175.8 0.2 multiply_reduce_fusion
  176.0 0.1 copy.81
  176.2 0.1 copy.62
  176.3 1.5 fusion.32
  177.8 0.9 copy.64
  178.6 3.6 %all-to-all-start.4 = ((bf16[8,32,1152]{2,1,0:T(8,128)(2,1)}), bf16[8,32,1152]{2,1,0:T(8,128)(2,1)S(1)}, u32[]{:S(2)}, u32[]{:S(2)}) async-start(bf16[8,32,1152]{2,1,0:T(8,128)(2,1)} %copy.64), calls=%async_computation.4 | async-start | bytes 1179648 | tf_op jit(solution)/shard_map/all_to_all | solution.py:106
  182.3 16.0 %all-to-all-done.4 = bf16[8,32,1152]{2,1,0:T(8,128)(2,1)S(1)} async-done(((bf16[8,32,1152]{2,1,0:T(8,128)(2,1)}), bf16[8,32,1152]{2,1,0:T(8,128)(2,1)S(1)}, u32[]{:S(2)}, u32[]{:S(2)}) %all-to-all-start.4) | async-done | bytes 589856 | tf_op jit(solution)/shard_map/all_to_all | solution.py:106
  198.3 0.4 fusion.45
  198.7 5.9 %fusion.33 = bf16[8,32,1152]{2,1,0:T(8,128)(2,1)S(1)} fusion(bf16[8,32,3072]{2,1,0:T(8,128)(2,1)} %get-tuple-element.9, bf16[3072,1152]{1,0:T(8,128)(2,1)} %param.17, bf16[8,32,1152]{2,1,0:T(8,128)(2,1)S(1)} %copy-done.1, f32[8,32,1152]{2,0,1:T(8,128)S(1)} %fusion.45, pred[8,32]{1,0:T(8,128)(4,1)S(1)} %copy-done.7), kind=kOutput, calls=%fused_computation.23 | convolution fusion | flops 1813413888 | bytes 11010304 | tf_op jit(solution)/shard_map/dot_general | solution.py:48
  204.6 0.6 gather_fusion
  205.2 0.2 fusion.59
  205.5 69.7 %all_gather.3 = bf16[256,1152]{1,0:T(8,128)(2,1)S(1)} all-gather(bf16[8,1152]{1,0:T(8,128)(2,1)S(1)} %fusion.61), channel_id=1, replica_groups=mesh['req'=4,'ad'=8] {'req','ad'}, dimensions={0}, use_global_device_ids=true | all-gather | bytes 608256 | tf_op jit(solution)/shard_map/all_gather | solution.py:113
  275.2 0.9 fusion.75
  276.1 36.9 %pmax.7 = f32[256]{0:T(256)S(1)} all-reduce(f32[256]{0:T(256)S(1)} %get-tuple-element.10), channel_id=1, replica_groups=mesh['req'=4,'ad'=8] {'req','ad'}, use_global_device_ids=true, to_apply=%region_6.7 | all-reduce | flops 256 | bytes 2048 | tf_op jit(solution)/shard_map/pmax | solution.py:118
  313.0 0.2 exponential_reduce_fusion
  313.2 21.1 %psum.14 = f32[256]{0:T(256)S(1)} all-reduce(f32[256]{0:T(256)S(1)} %exponential_reduce_fusion), channel_id=1, replica_groups=mesh['req'=4,'ad'=8] {'ad'}, use_global_device_ids=true, to_apply=%region_8.9 | all-reduce | flops 256 | bytes 2048 | tf_op jit(solution)/shard_map/psum | solution.py:119
  334.3 5.9 %psum.15 = f32[256]{0:T(256)S(1)} all-reduce(f32[256]{0:T(256)S(1)} %psum.14), channel_id=1, replica_groups=mesh['req'=4,'ad'=8] {'req'}, use_global_device_ids=true, to_apply=%region_9.10 | all-reduce | flops 256 | bytes 2048 | tf_op jit(solution)/shard_map/psum | solution.py:119
  340.2 1.0 subtract_subtract_fusion
  (38 shorter events, 0.3 us)
Async XLA Ops:
  0.6 274.6 %copy-start = (bf16[1152,1000]{0,1:T(8,128)(2,1)S(1)}, bf16[1152,1000]{0,1:T(8,128)(2,1)}, u32[]{:S(2)}) copy-start(bf16[1152,1000]{0,1:T(8,128)(2,1)} %param.23) | copy-start | bytes 6912004
  2.2 13.6 %all-to-all-start.1 = ((s32[8,1,32]{2,1,0:T(1,128)}), s32[8,1,32]{2,1,0:T(1,128)S(1)}, u32[]{:S(2)}, u32[]{:S(2)}) async-start(s32[8,1,32]{2,1,0:T(1,128)} %broadcast_in_dim.35), calls=%async_computation.1 | async-start | bytes 8192 | tf_op jit(solution)/shard_map/all_to_all | solution.py:92
  11.5 110.6 %copy-start.6 = (pred[8,32]{1,0:T(8,128)(4,1)}, pred[8,32]{1,0:T(8,128)(4,1)S(1)}, u32[]{:S(2)}) copy-start(pred[8,32]{1,0:T(8,128)(4,1)S(1)} %iota_compare_fusion.2) | copy-start | bytes 772
  11.5 24.2 %copy-start.8 = (bf16[4,32,1152]{2,1,0:T(8,128)(2,1)S(1)}, bf16[4,32,1152]{2,1,0:T(8,128)(2,1)}, u32[]{:S(2)}) copy-start(bf16[4,32,1152]{2,1,0:T(8,128)(2,1)} %param.18) | copy-start | bytes 884740
  13.3 24.1 %copy-start.2 = (bf16[4,2,16,3072]{3,2,1,0:T(8,128)(2,1)S(1)}, bf16[4,2,16,3072]{3,2,1,0:T(8,128)(2,1)}, u32[]{:S(2)}) copy-start(bf16[4,2,16,3072]{3,2,1,0:T(8,128)(2,1)} %param.19) | copy-start | bytes 2359300
  15.9 19.8 %all-to-all-start = ((bf16[8,32,1152]{2,1,0:T(8,128)(2,1)}), bf16[8,32,1152]{2,1,0:T(8,128)(2,1)}, u32[]{:S(2)}, u32[]{:S(2)}) async-start(bf16[8,32,1152]{2,1,0:T(8,128)(2,1)} %copy.48), calls=%async_computation | async-start | bytes 1179648 | tf_op jit(solution)/shard_map/all_to_all | solution.py:91
  38.4 78.9 %slice-start = ((s8[14155776]{0:T(1024)(128)(4,1)}), s8[4194304]{0:T(1024)(128)(4,1)S(1)}, s32[]{:S(2)}) async-start(s8[14155776]{0:T(1024)(128)(4,1)} %bitcast.88), calls=%async_computation.5 | async-start | bytes 8388608
  38.7 78.6 %slice-start.1 = ((s8[14155776]{0:T(1024)(128)(4,1)}), s8[4194304]{0:T(1024)(128)(4,1)S(1)}, s32[]{:S(2)}) async-start(s8[14155776]{0:T(1024)(128)(4,1)} %bitcast.88), calls=%async_computation.6 | async-start | bytes 8388608
  113.0 4.3 %slice-start.2 = ((s8[14155776]{0:T(1024)(128)(4,1)}), s8[4194304]{0:T(1024)(128)(4,1)S(1)}, s32[]{:S(2)}) async-start(s8[14155776]{0:T(1024)(128)(4,1)} %bitcast.88), calls=%async_computation.7 | async-start | bytes 8388608
  116.5 1.1 copy-start.1
  116.5 1.1 copy-start.4
  116.6 1.6 slice-start.3
  130.4 40.4 %all-to-all-start.3 = ((bf16[8,32,3072]{2,1,0:T(8,128)(2,1)}), bf16[8,32,3072]{2,1,0:T(8,128)(2,1)}, u32[]{:S(2)}, u32[]{:S(2)}) async-start(bf16[8,32,3072]{2,1,0:T(8,128)(2,1)} %copy.58), calls=%async_computation.3 | async-start | bytes 3145728 | tf_op jit(solution)/shard_map/all_to_all | solution.py:103
  176.3 6.0 %copy-start.9 = (s32[8]{0:T(128)S(1)}, s32[8]{0:T(128)}, u32[]{:S(2)}) copy-start(s32[8]{0:T(128)} %param.13) | copy-start | bytes 100
  177.8 20.9 %copy-start.7 = (pred[8,32]{1,0:T(8,128)(4,1)S(1)}, pred[8,32]{1,0:T(8,128)(4,1)}, u32[]{:S(2)}) copy-start(pred[8,32]{1,0:T(8,128)(4,1)} %copy-done.6) | copy-start | bytes 772
  178.6 19.6 %all-to-all-start.4 = ((bf16[8,32,1152]{2,1,0:T(8,128)(2,1)}), bf16[8,32,1152]{2,1,0:T(8,128)(2,1)S(1)}, u32[]{:S(2)}, u32[]{:S(2)}) async-start(bf16[8,32,1152]{2,1,0:T(8,128)(2,1)} %copy.64), calls=%async_computation.4 | async-start | bytes 1179648 | tf_op jit(solution)/shard_map/all_to_all | solution.py:106
  198.7 6.8 %copy-start.5 = (f32[1152]{0:T(1024)S(1)}, f32[1152]{0:T(1024)}, u32[]{:S(2)}) copy-start(f32[1152]{0:T(1024)} %param.22) | copy-start | bytes 13828
  204.6 0.9 copy-start.3
